TPU v7x, 32 devices: a whole 2x2x4 slice. The times are simulated.
32 devices in a mesh: grp: 2 (over y), blk: 4 (over z), head: 2 (over x), sub: 2 (over core).
Axes of the slice: x: 2, y: 2, z: 4, core: 2. Of those that a mesh axis runs over, the one named last changes fastest.
Arguments:
- queries: bfloat16 [4096, 4096], P(('grp', 'blk', 'head', 'sub')), parts along dimension 0, may hold values from -46 to 46
- keys: bfloat16 [4096, 4096], P(('grp', 'blk', 'head', 'sub')), parts along dimension 0, may hold values from -4 to 4
- values: bfloat16 [4096, 4096], P(('grp', 'blk', 'head', 'sub')), parts along dimension 0, may hold values from -6 to 6
- block_lists: int32 [32, 16, 8], replicated, may hold values from 0 to 15, as said below
Outputs:
- attended: bfloat16 [4096, 4096], P(('grp', 'blk', 'head', 'sub')), parts along dimension 0
There are 2 independent parts, one for each index of `grp`. A program takes and returns all parts, laid end to end along the dimension named above; an argument that names none is the same for every part. Nothing has to cross between parts.
Inputs may be any that keep to these rules, and one draw needn't show every extreme that they name: `block_lists`: the first entry of every list is the query tile itself; entries may repeat. Tiles are numbered frame by frame, 4 to a frame. In each head either all entries lie in the query tile's frame or the frames next to it, or all entries have the query tile's position within its frame.
All inputs are finite; a program needn't handle non-finite values.
Results may differ from a plain program's by a relative error of at most 0.0065.
Values may be sent and summed in bfloat16 or wider, within the bound.
A program may use at most 64 MiB of HBM per device.

v0:
```python
import functools
import math

import jax
import jax.numpy as jnp
from jax import lax
from jax.experimental import pallas as pl
from jax.experimental.pallas import tpu as pltpu
from jax.sharding import PartitionSpec as P

HEADS = 32
HEAD_DIM = 128
TILE = 128


NEG_FLOOR = -1e30


def query_rows(block_lists, first_head, heads_here, query_tokens):
    tile_ids = jnp.arange(block_lists.shape[1], dtype=jnp.int32)
    lists_local = lax.dynamic_slice_in_dim(block_lists, first_head, heads_here, 0)
    tile_mask = jnp.any(lists_local[:, :, :, None] == tile_ids, axis=2).astype(jnp.bfloat16)
    query_onehot = ((query_tokens // TILE)[:, None] == tile_ids[None, :]).astype(jnp.bfloat16)
    listed = jnp.einsum("qi,hij->hqj", query_onehot, tile_mask, preferred_element_type=jnp.float32)
    return listed.astype(jnp.bfloat16)


def attend_block(state_now, key_block, value_block, allowed, query_local, score_scale):
    top_old, total_old, accum_old = state_now
    scores = (
        jnp.einsum("qhd,khd->hqk", query_local, key_block, preferred_element_type=jnp.float32)
        * score_scale
    )
    top_new = jnp.maximum(top_old, jnp.max(jnp.where(allowed, scores, NEG_FLOOR), axis=2))
    factor = jnp.exp(top_old - top_new)
    weights = jnp.where(allowed, jnp.exp(scores - top_new[:, :, None]), 0.0)
    total_new = total_old * factor + jnp.sum(weights, axis=2)
    product = jnp.einsum(
        "hqk,khd->qhd",
        weights.astype(jnp.bfloat16),
        value_block,
        preferred_element_type=jnp.float32,
    )
    accum_new = accum_old * jnp.transpose(factor)[:, :, None] + product
    return (top_new, total_new, accum_new)


def make_step(query_local, listed_rows, key_token, block_len, tile_total):
    score_scale = 1.0 / math.sqrt(HEAD_DIM)
    tile_ids = jnp.arange(tile_total, dtype=jnp.int32)

    def fold_step(state_now, piece, first_row):
        key_piece, value_piece = piece
        block_count = key_piece.shape[0] // block_len

        def one_block(block_index, state_in):
            key_block = lax.dynamic_slice_in_dim(key_piece, block_index * block_len, block_len, 0)
            value_block = lax.dynamic_slice_in_dim(
                value_piece, block_index * block_len, block_len, 0
            )
            positions = block_index * block_len + jnp.arange(block_len, dtype=jnp.int32)
            key_tiles = key_token(positions) // TILE
            key_onehot = (tile_ids[:, None] == key_tiles[None, :]).astype(jnp.bfloat16)
            allowed = (
                jnp.einsum(
                    "hqj,jk->hqk", listed_rows, key_onehot, preferred_element_type=jnp.float32
                )
                > 0.5
            )
            result = attend_block(
                state_in, key_block, value_block, allowed, query_local, score_scale
            )
            return result

        return lax.fori_loop(0, block_count, one_block, state_now)

    return fold_step


def start_state(heads_here, block_len):
    top_all = jnp.full((heads_here, block_len), NEG_FLOOR, jnp.float32)
    total_all = jnp.zeros((heads_here, block_len), jnp.float32)
    accum_all = jnp.zeros((block_len, heads_here, HEAD_DIM), jnp.float32)
    return (top_all, total_all, accum_all)


def normalize(state_end):
    top_all, total_all, accum_all = state_end
    return (accum_all / jnp.transpose(total_all)[:, :, None]).astype(jnp.bfloat16)


def per_device(queries, keys, values, block_lists):
    row_count, col_count = queries.shape
    n_head = lax.axis_size("head")
    n_sub = lax.axis_size("sub")
    blk_index = lax.axis_index("blk")
    head_index = lax.axis_index("head")
    sub_index = lax.axis_index("sub")
    tile_total = block_lists.shape[1]
    heads_here = HEADS // (n_head * n_sub)
    block_len = row_count * n_head * n_sub

    def inward(tensor):
        return tensor.reshape(1, 1, row_count, n_head, n_sub, heads_here * HEAD_DIM)

    query_six, keys_six, values_six = (
        lax.all_to_all(
            lax.all_to_all(inward(queries), "head", split_axis=3, concat_axis=1, tiled=True),
            "sub",
            split_axis=4,
            concat_axis=0,
            tiled=True,
        ),
        lax.all_to_all(
            lax.all_to_all(inward(keys), "head", split_axis=3, concat_axis=1, tiled=True),
            "sub",
            split_axis=4,
            concat_axis=0,
            tiled=True,
        ),
        lax.all_to_all(
            lax.all_to_all(inward(values), "head", split_axis=3, concat_axis=1, tiled=True),
            "sub",
            split_axis=4,
            concat_axis=0,
            tiled=True,
        ),
    )
    query_local = query_six.reshape(block_len, heads_here, HEAD_DIM)
    keys_local = keys_six.reshape(block_len, heads_here, HEAD_DIM)
    values_local = values_six.reshape(block_len, heads_here, HEAD_DIM)

    def key_token(positions):
        source_dev = positions // block_len
        within = positions % block_len
        sub_source = within // (n_head * row_count)
        head_source = within // row_count % n_head
        offset = within % row_count
        return ((source_dev * n_head + head_source) * n_sub + sub_source) * row_count + offset

    query_tokens = key_token(blk_index * block_len + jnp.arange(block_len, dtype=jnp.int32))
    first_head = (head_index * n_sub + sub_index) * heads_here
    listed_rows = query_rows(block_lists, first_head, heads_here, query_tokens)
    fold_step = make_step(query_local, listed_rows, key_token, block_len, tile_total)
    state_end = fold_step(
        start_state(heads_here, block_len),
        (
            lax.all_gather(keys_local, "blk", axis=0, tiled=True),
            lax.all_gather(values_local, "blk", axis=0, tiled=True),
        ),
        jnp.int32(0),
    )
    result_rows = normalize(state_end)
    attended = result_rows.reshape(n_sub, n_head, row_count, 1, 1, heads_here * HEAD_DIM)
    returned = lax.all_to_all(
        lax.all_to_all(attended, "head", split_axis=1, concat_axis=3, tiled=True),
        "sub",
        split_axis=0,
        concat_axis=4,
        tiled=True,
    )
    return returned.reshape(row_count, col_count)


NEAR_COUNTS = (0, 8, 12, 16, 20)


def attend_tile(ids, query, buf, first):
    score_scale = 1.0 / math.sqrt(HEAD_DIM)
    scores, top = [], None
    for tile in ids:
        s = lax.dot_general(
            query, buf[first, tile], (((1,), (1,)), ((), ())), preferred_element_type=jnp.float32
        ) * score_scale
        scores.append(s)
        top = s if top is None else jnp.maximum(top, s)
    row_top = jnp.max(top, axis=1, keepdims=True)
    total, accum = None, None
    for e, tile in enumerate(ids):
        w = jnp.exp(scores[e] - row_top)
        if e:
            repeat = tile == ids[0]
            for f in range(1, e):
                repeat = jnp.logical_or(repeat, tile == ids[f])
            w = w * jnp.where(repeat, 0.0, 1.0)
        part = jnp.dot(
            w.astype(jnp.bfloat16), buf[first + 1, tile], preferred_element_type=jnp.float32
        )
        total = w if total is None else total + w
        accum = part if accum is None else accum + part
    row_total = jnp.sum(total, axis=1, keepdims=True)
    return (accum / row_total).astype(jnp.bfloat16)


def exchange_kernel(sizes, entries, near, stage, list_rows, landed, lists, list_sem, *scratch):
    n_blk, n_head, n_sub = sizes
    line_count = n_head * n_sub
    count = n_blk * line_count
    near_here = near // line_count
    far = HEADS - near
    far_here = -(-far // count)
    far_in = scratch[:far_here]
    far_out = scratch[far_here : 2 * far_here]
    scratch = scratch[2 * far_here :]
    near_query = scratch[:near_here]
    near_kv = scratch[near_here : 2 * near_here]
    near_out = scratch[2 * near_here : 3 * near_here]
    far_send, far_recv, far_local = scratch[3 * near_here : 3 * near_here + 3]
    if near:
        near_send, near_recv, near_local, hop_send, hop_recv = scratch[3 * near_here + 3 :]

    blk = lax.axis_index("blk")
    line = lax.axis_index("head") * n_sub + lax.axis_index("sub")
    me = blk * line_count + line

    def remote(src, dst, send, recv, rank):
        return pltpu.make_async_remote_copy(
            src_ref=src,
            dst_ref=dst,
            send_sem=send,
            recv_sem=recv,
            device_id={
                "blk": rank // line_count,
                "head": rank // n_sub % n_head,
                "sub": rank % n_sub,
            },
            device_id_type=pl.DeviceIdType.MESH,
        )

    def peer(d):
        return (me + d) % count

    def line_peer(d):
        return (line + d) % line_count

    def far_number(rank, a):
        turn = (rank % line_count + count - rank // line_count) % line_count
        return a * count + rank // line_count + n_blk * turn

    def far_inward(t, a, target, sender):
        return remote(
            stage.at[t, near + far_number(target, a)], far_in[a].at[t, sender],
            far_send.at[t, a, target], far_recv.at[t, a, sender], target,
        )

    def far_outward(a, target, sender):
        return remote(
            far_out[a].at[target], landed.at[near + far_number(sender, a)],
            far_send.at[3, a, target], far_recv.at[3, a, sender], target,
        )

    def far_own_in(t, a):
        return pltpu.make_async_copy(
            stage.at[t, near + far_number(me, a)], far_in[a].at[t, me], far_local.at[t, a]
        )

    def far_own_out(a):
        return pltpu.make_async_copy(
            far_out[a].at[me], landed.at[near + far_number(me, a)], far_local.at[3, a]
        )

    def if_far(rank, a, action):
        if (a + 1) * count <= far:
            action()
        else:
            pl.when(far_number(rank, a) < far)(action)

    def near_slot(t, a, sender):
        if t == 0:
            return near_query[a].at[sender]
        return near_kv[a].at[t - 1, line_count + sender]

    def near_inward(t, a, target, sender):
        return remote(
            stage.at[t, a * line_count + target], near_slot(t, a, sender),
            near_send.at[t, a, target], near_recv.at[t, a, sender], blk * line_count + target,
        )

    def near_outward(a, target, sender):
        return remote(
            near_out[a].at[target], landed.at[a * line_count + sender],
            near_send.at[3, a, target], near_recv.at[3, a, sender], blk * line_count + target,
        )

    def near_own_in(t, a):
        return pltpu.make_async_copy(
            stage.at[t, a * line_count + line], near_slot(t, a, line), near_local.at[t, a]
        )

    def near_own_out(a):
        return pltpu.make_async_copy(
            near_out[a].at[line], landed.at[a * line_count + line], near_local.at[3, a]
        )

    def hop(a, direction):
        return remote(
            near_kv[a].at[:, pl.ds(line_count, line_count)],
            near_kv[a].at[:, pl.ds(2 * line_count * direction, line_count)],
            hop_send.at[a, direction], hop_recv.at[a, direction],
            (me + line_count if direction == 0 else me + count - line_count) % count,
        )

    def each_hop(action, sending):
        up, down = blk < n_blk - 1, blk > 0
        pl.when(up if sending else down)(functools.partial(action, 0))
        pl.when(down if sending else up)(functools.partial(action, 1))

    barrier = pltpu.get_barrier_semaphore()

    def greet(d, carry):
        rank = peer(d)
        pl.semaphore_signal(
            barrier, inc=1,
            device_id={
                "blk": rank // line_count,
                "head": rank // n_sub % n_head,
                "sub": rank % n_sub,
            },
            device_id_type=pl.DeviceIdType.MESH,
        )
        return carry

    lax.fori_loop(1, count, greet, 0)

    def own_list(a, far_head):
        slot = near + far_number(me, a) if far_head else a * line_count + line
        row = near_here + a if far_head else a
        return pltpu.make_async_copy(list_rows.at[slot], lists.at[row], list_sem.at[row])

    for a in range(near_here):
        own_list(a, False).start()
    for a in range(far_here):
        if_far(me, a, lambda a=a: own_list(a, True).start())
    pl.semaphore_wait(barrier, count - 1)

    for a in range(near_here):
        def near_send_in(d, carry, a=a):
            for t in (1, 2, 0):
                near_inward(t, a, line_peer(d), line).start()
            return carry

        lax.fori_loop(1, line_count, near_send_in, 0)
        for t in range(3):
            near_own_in(t, a).start()

    for a in range(far_here):
        def far_send_in(d, carry, a=a):
            def send(d=d):
                for t in range(3):
                    far_inward(t, a, peer(d), me).start()

            if_far(peer(d), a, send)
            return carry

        lax.fori_loop(1, count, far_send_in, 0)

        def own(a=a):
            for t in range(3):
                far_own_in(t, a).start()

        if_far(me, a, own)

    for a in range(near_here):
        for t in range(3):
            near_own_in(t, a).wait()

        def near_arrive(d, carry, a=a):
            for t in range(3):
                near_inward(t, a, line, line_peer(d)).wait_recv()
            return carry

        lax.fori_loop(1, line_count, near_arrive, 0)
        each_hop(lambda direction, a=a: hop(a, direction).start(), True)

    for a in range(far_here):
        def far_whole(a=a):
            for t in range(3):
                far_own_in(t, a).wait()

            def far_arrive(d, carry):
                for t in range(3):
                    far_inward(t, a, me, peer(d)).wait_recv()
                return carry

            lax.fori_loop(1, count, far_arrive, 0)
            own_list(a, True).wait()

            def one(i):
                ids = [lists[near_here + a, i * entries + e] for e in range(entries)]
                far_out[a][i] = attend_tile(ids, far_in[a][0, i], far_in[a], 1)

            def work(d, carry):
                one(peer(d))

                @pl.when(d > 1)
                def _():
                    far_outward(a, peer(d - 1), me).start()

                return carry

            lax.fori_loop(1, count, work, 0)
            one(me)
            far_outward(a, peer(count - 1), me).start()
            far_own_out(a).start()

        if_far(me, a, far_whole)

    for a in range(near_here):
        each_hop(lambda direction, a=a: hop(a, direction).wait_recv(), False)
        own_list(a, False).wait()

        def one(i, a=a):
            tile = blk * line_count + i
            first = (blk - 1) * line_count
            ids = [
                jnp.clip(lists[a, tile * entries + e] - first, 0, 3 * line_count - 1) for e in range(entries)
            ]
            near_out[a][i] = attend_tile(ids, near_query[a][i], near_kv[a], 0)

        def work(d, carry, a=a, one=one):
            one(line_peer(d))

            @pl.when(d > 1)
            def _():
                near_outward(a, line_peer(d - 1), line).start()

            return carry

        lax.fori_loop(1, line_count, work, 0)
        one(line)
        near_outward(a, line_peer(line_count - 1), line).start()
        near_own_out(a).start()

    for a in range(far_here):
        def finish_own(a=a):
            far_own_out(a).wait()

            def sent_back(d, carry):
                far_outward(a, peer(d), me).wait_send()
                return carry

            lax.fori_loop(1, count, sent_back, 0)

        if_far(me, a, finish_own)

        def finish(d, carry, a=a):
            def other(d=d):
                for t in range(3):
                    far_inward(t, a, peer(d), me).wait_send()
                far_outward(a, me, peer(d)).wait_recv()

            if_far(peer(d), a, other)
            return carry

        lax.fori_loop(1, count, finish, 0)

    for a in range(near_here):
        near_own_out(a).wait()
        each_hop(lambda direction, a=a: hop(a, direction).wait_send(), True)

        def near_finish(d, carry, a=a):
            for t in range(3):
                near_inward(t, a, line_peer(d), line).wait_send()
            near_outward(a, line_peer(d), line).wait_send()
            near_outward(a, line, line_peer(d)).wait_recv()
            return carry

        lax.fori_loop(1, line_count, near_finish, 0)


def restore_kernel(place, landed, out_ref):
    for h in range(HEADS):
        out_ref[:, h * HEAD_DIM : (h + 1) * HEAD_DIM] = landed[place[h]]


def arrange_kernel(frames, line_count, nears, lists_ref, q_ref, k_ref, v_ref, stage, list_rows,
                   place_out, choice_out, order, order_scalar, order_sem):
    @pl.when(pl.program_id(0) == 0)
    def _():
        ids = lists_ref[...]
        steps, heads = ids.shape
        per_frame = steps // frames
        away = None
        for f in range(frames):
            part = ids[f * per_frame : (f + 1) * per_frame]
            outside = jnp.logical_or(
                part < (f - 1) * line_count, part >= (f + 2) * line_count
            )
            found = jnp.max(jnp.where(outside, 1, 0), axis=0, keepdims=True)
            away = found if away is None else jnp.maximum(away, found)
        row = lax.broadcasted_iota(jnp.int32, (heads, heads), 0)
        col = lax.broadcasted_iota(jnp.int32, (heads, heads), 1)
        away_col = jnp.broadcast_to(away, (heads, heads))
        away_row = jnp.broadcast_to(
            jnp.sum(jnp.where(row == col, away_col, 0), axis=1, keepdims=True), (heads, heads)
        )
        same = away_row == away_col
        ahead = jnp.where(same, jnp.where(row < col, 1, 0), away_col)
        place = jnp.sum(ahead, axis=0, keepdims=True)
        picks = jnp.broadcast_to(place, (heads, heads)) == row
        behind = jnp.where(same, jnp.where(col < row, 1, 0), away_row)
        place_of_row = jnp.sum(behind, axis=1, keepdims=True)
        perm = jnp.sum(
            jnp.where(jnp.broadcast_to(place_of_row, (heads, heads)) == col, row, 0),
            axis=0, keepdims=True,
        )
        near_total = heads - jnp.sum(away, axis=1, keepdims=True)
        choice = jnp.zeros((1, 1), jnp.int32)
        for n in nears[1:]:
            choice = choice + jnp.where(near_total >= n, 1, 0)
        order[0:1, 0:heads] = perm
        order[1:2, 0:heads] = place
        order[2:3, 0:heads] = jnp.broadcast_to(choice, (1, heads))
        copy = pltpu.make_async_copy(order, order_scalar, order_sem)
        copy.start()
        rows_now = lax.dot_general(
            jnp.where(picks, 1.0, 0.0).astype(jnp.bfloat16),
            ids.astype(jnp.float32).astype(jnp.bfloat16),
            (((1,), (1,)), ((), ())),
            preferred_element_type=jnp.float32,
        )
        list_rows[...] = rows_now.astype(jnp.int32)
        copy.wait()
        for h in range(heads):
            place_out[h] = order_scalar[1, h]
        choice_out[0] = order_scalar[2, 0]

    for slot in range(HEADS):
        columns = pl.ds(pl.multiple_of(order_scalar[0, slot] * HEAD_DIM, HEAD_DIM), HEAD_DIM)
        for t, source in enumerate((q_ref, k_ref, v_ref)):
            stage[t, slot] = source[:, columns]


def arrange(line_count, nears, queries, keys, values, block_lists):
    rows, width = queries.shape
    heads, tiles, entries = block_lists.shape
    steps = 4
    part = rows // steps
    block = pl.BlockSpec((part, width), lambda i: (i, 0))
    by_row = jnp.transpose(block_lists, (1, 2, 0)).reshape(tiles * entries, heads)
    smem = pl.BlockSpec(memory_space=pltpu.SMEM)
    return pl.pallas_call(
        functools.partial(arrange_kernel, tiles // line_count, line_count, nears),
        grid=(steps,),
        out_shape=(
            jax.ShapeDtypeStruct((3, HEADS, rows, HEAD_DIM), jnp.bfloat16),
            jax.ShapeDtypeStruct((heads, tiles * entries), jnp.int32),
            jax.ShapeDtypeStruct((heads,), jnp.int32),
            jax.ShapeDtypeStruct((1,), jnp.int32),
        ),
        in_specs=[pl.BlockSpec(by_row.shape, lambda i: (0, 0)), block, block, block],
        out_specs=(
            pl.BlockSpec((3, HEADS, part, HEAD_DIM), lambda i: (0, 0, i, 0)),
            pl.BlockSpec((heads, tiles * entries), lambda i: (0, 0)),
            smem,
            smem,
        ),
        scratch_shapes=[
            pltpu.VMEM((8, 128), jnp.int32),
            pltpu.SMEM((8, 128), jnp.int32),
            pltpu.SemaphoreType.DMA,
        ],
    )(by_row, queries, keys, values)


def whole_exchange(sizes, entries, near, collective_id, stage, list_rows, place):
    line_count = sizes[1] * sizes[2]
    count = sizes[0] * line_count
    near_here = near // line_count
    far_here = -(-(HEADS - near) // count)
    rows = stage.shape[2]
    block = (rows, HEAD_DIM)
    anywhere = pl.BlockSpec(memory_space=pl.ANY)
    smem = pl.BlockSpec(memory_space=pltpu.SMEM)
    vmem = pl.BlockSpec(memory_space=pltpu.VMEM)
    dma = pltpu.SemaphoreType.DMA
    rows_here = near_here + far_here
    scratch = [pltpu.SMEM((rows_here,) + list_rows.shape[1:], jnp.int32), dma((rows_here,))]
    scratch += [pltpu.VMEM((3, count) + block, jnp.bfloat16)] * far_here
    scratch += [pltpu.VMEM((count,) + block, jnp.bfloat16)] * far_here
    scratch += [pltpu.VMEM((line_count,) + block, jnp.bfloat16)] * near_here
    scratch += [pltpu.VMEM((2, 3 * line_count) + block, jnp.bfloat16)] * near_here
    scratch += [pltpu.VMEM((line_count,) + block, jnp.bfloat16)] * near_here
    scratch += [dma((4, far_here, count))] * 2 + [dma((4, far_here))]
    if near:
        scratch += [dma((4, near_here, line_count))] * 2 + [dma((4, near_here))]
        scratch += [dma((near_here, 2))] * 2
    landed = pl.pallas_call(
        functools.partial(exchange_kernel, sizes, entries, near),
        out_shape=jax.ShapeDtypeStruct((HEADS,) + block, jnp.bfloat16),
        in_specs=[anywhere, anywhere],
        out_specs=anywhere,
        scratch_shapes=scratch,
        compiler_params=pltpu.CompilerParams(
            collective_id=collective_id, has_side_effects=True
        ),
    )(stage, list_rows)
    return pl.pallas_call(
        restore_kernel,
        out_shape=jax.ShapeDtypeStruct((rows, HEADS * HEAD_DIM), jnp.bfloat16),
        in_specs=[smem, vmem],
        out_specs=vmem,
    )(place, landed)


def solution(mesh):
    sizes = tuple(mesh.shape[axis] for axis in ("blk", "head", "sub"))
    line_count = sizes[1] * sizes[2]
    count = sizes[0] * line_count

    def body(queries, keys, values, block_lists):
        if queries.shape[0] != TILE or HEADS % count or block_lists.shape[1] != count:
            return per_device(queries, keys, values, block_lists)
        nears = [n for n in NEAR_COUNTS if n % line_count == 0 and n < HEADS]
        stage, list_rows, place, choice = arrange(
            line_count, nears, queries, keys, values, block_lists
        )
        branches = [
            functools.partial(whole_exchange, sizes, block_lists.shape[2], n, number)
            for number, n in enumerate(nears)
        ]
        return lax.switch(choice[0], branches, stage, list_rows, place)

    in_specs = (
        P(("grp", "blk", "head", "sub"), None),
        P(("grp", "blk", "head", "sub"), None),
        P(("grp", "blk", "head", "sub"), None),
        P(),
    )
    out_specs = P(("grp", "blk", "head", "sub"), None)
    return jax.shard_map(
        body, mesh=mesh, in_specs=in_specs, out_specs=out_specs, check_vma=False
    )
```

profile of v0, /device:TPU:11, one launch (start us, length us, event | category | flops | bytes accessed | tf_op | source)
XLA Modules:
  0.0 85.9 jit_solution(4854159469224245946)
XLA Ops:
  0.0 4.7 %shard_map.51 = (bf16[3,32,128,128]{3,2,1,0:T(8,128)(2,1)S(1)}, s32[32,128]{1,0:T(8,128)S(1)}, s32[32]{0:T(128)S(1)}, s32[1]{0:T(128)}) custom-call(s32[128,32]{1,0:T(8,128)} %bitcast.4, bf16[128,4096]{1,0:T(8,128)(2,1)} %q_ref.1, bf16[128,4096]{1,0:T(8,128)(2,1)} %k_ref.1, bf16[128,4096]{1,0:T(8,128)(2,1)} %v_ref.1), custom_call_target="tpu_custom_call" | custom-call | tf_op jit(solution)/shard_map/pallas_call | solution.py:542
  5.4 79.6 %conditional.1 = (bf16[128,4096]{1,0:T(8,128)(2,1)S(1)}) conditional(s32[]{:T(128)} %bitcast.2, (bf16[3,32,128,128]{3,2,1,0:T(8,128)(2,1)S(1)}, s32[32,128]{1,0:T(8,128)S(1)}, s32[32]{0:T(128)S(1)}) %tuple.20, (bf16[3,32,128,128]{3,2,1,0:T(8,128)(2,1)S(1)}, s32[32,128]{1,0:T(8,128)S(1)}, s32[32]{0:T(128)S(1)}) %tuple.20, ...), branch_computations={%region_0.0_spmd, %region_1.0_spmd, %region_2.0_spmd, %region_3.0_... | conditional | bytes 8 | solution.py:622
  5.6 77.5 %branch_3_fun.2.landed = bf16[32,128,128]{2,1,0:T(8,128)(2,1)} custom-call(bf16[3,32,128,128]{3,2,1,0:T(8,128)(2,1)S(1)} %get-tuple-element.51.stage, s32[32,128]{1,0:T(8,128)S(1)} %get-tuple-element.52.list_rows), custom_call_target="tpu_custom_call" | custom-call | tf_op jit(solution)/shard_map/cond/branch_3_fun/pallas_call | solution.py:588
  83.2 1.5 %branch_3_fun.3 = bf16[128,4096]{1,0:T(8,128)(2,1)S(1)} custom-call(s32[32]{0:T(128)S(1)} %get-tuple-element.50.place, bf16[32,128,128]{2,1,0:T(8,128)(2,1)} %branch_3_fun.2.landed), custom_call_target="tpu_custom_call" | custom-call | tf_op jit(solution)/shard_map/cond/branch_3_fun/pallas_call | solution.py:598
  85.0 0.0 copy-start
  85.0 1.0 %copy-done = bf16[128,4096]{1,0:T(8,128)(2,1)} copy-done((bf16[128,4096]{1,0:T(8,128)(2,1)}, bf16[128,4096]{1,0:T(8,128)(2,1)S(1)}, u32[]{:S(2)}) %copy-start) | copy-done | bytes 1048600
Async XLA Ops:
  85.0 1.0 %copy-start = (bf16[128,4096]{1,0:T(8,128)(2,1)}, bf16[128,4096]{1,0:T(8,128)(2,1)S(1)}, u32[]{:S(2)}) copy-start(bf16[128,4096]{1,0:T(8,128)(2,1)S(1)} %get-tuple-element.70) | copy-start | bytes 3145732
where the time goes:
time: 86.1 us; the launch traced here: 85.9 us
  Pallas kernels  83.8 us (97%)
  local copies, waits for them, and re-layouts  0.96 us (1%)
    pallas_call x1, Pallas kernels, whole_exchange(): pl.pallas_call(functools.partial(exchange_kernel, sizes, entries, near),...  77.5 us
    pallas_call x1, Pallas kernels, arrange(): pl.pallas_call(functools.partial(arrange_kernel, tiles // line_count, lin...  4.71 us

commit v1 on v0

v1 whole, which is shorter than its diff:
```python
import functools
import math

import jax
import jax.numpy as jnp
from jax import lax
from jax.experimental import pallas as pl
from jax.experimental.pallas import tpu as pltpu
from jax.sharding import PartitionSpec as P

HEADS = 32
HEAD_DIM = 128
TILE = 128


NEG_FLOOR = -1e30


def query_rows(block_lists, first_head, heads_here, query_tokens):
    tile_ids = jnp.arange(block_lists.shape[1], dtype=jnp.int32)
    lists_local = lax.dynamic_slice_in_dim(block_lists, first_head, heads_here, 0)
    tile_mask = jnp.any(lists_local[:, :, :, None] == tile_ids, axis=2).astype(jnp.bfloat16)
    query_onehot = ((query_tokens // TILE)[:, None] == tile_ids[None, :]).astype(jnp.bfloat16)
    listed = jnp.einsum("qi,hij->hqj", query_onehot, tile_mask, preferred_element_type=jnp.float32)
    return listed.astype(jnp.bfloat16)


def attend_block(state_now, key_block, value_block, allowed, query_local, score_scale):
    top_old, total_old, accum_old = state_now
    scores = (
        jnp.einsum("qhd,khd->hqk", query_local, key_block, preferred_element_type=jnp.float32)
        * score_scale
    )
    top_new = jnp.maximum(top_old, jnp.max(jnp.where(allowed, scores, NEG_FLOOR), axis=2))
    factor = jnp.exp(top_old - top_new)
    weights = jnp.where(allowed, jnp.exp(scores - top_new[:, :, None]), 0.0)
    total_new = total_old * factor + jnp.sum(weights, axis=2)
    product = jnp.einsum(
        "hqk,khd->qhd",
        weights.astype(jnp.bfloat16),
        value_block,
        preferred_element_type=jnp.float32,
    )
    accum_new = accum_old * jnp.transpose(factor)[:, :, None] + product
    return (top_new, total_new, accum_new)


def make_step(query_local, listed_rows, key_token, block_len, tile_total):
    score_scale = 1.0 / math.sqrt(HEAD_DIM)
    tile_ids = jnp.arange(tile_total, dtype=jnp.int32)

    def fold_step(state_now, piece, first_row):
        key_piece, value_piece = piece
        block_count = key_piece.shape[0] // block_len

        def one_block(block_index, state_in):
            key_block = lax.dynamic_slice_in_dim(key_piece, block_index * block_len, block_len, 0)
            value_block = lax.dynamic_slice_in_dim(
                value_piece, block_index * block_len, block_len, 0
            )
            positions = block_index * block_len + jnp.arange(block_len, dtype=jnp.int32)
            key_tiles = key_token(positions) // TILE
            key_onehot = (tile_ids[:, None] == key_tiles[None, :]).astype(jnp.bfloat16)
            allowed = (
                jnp.einsum(
                    "hqj,jk->hqk", listed_rows, key_onehot, preferred_element_type=jnp.float32
                )
                > 0.5
            )
            result = attend_block(
                state_in, key_block, value_block, allowed, query_local, score_scale
            )
            return result

        return lax.fori_loop(0, block_count, one_block, state_now)

    return fold_step


def start_state(heads_here, block_len):
    top_all = jnp.full((heads_here, block_len), NEG_FLOOR, jnp.float32)
    total_all = jnp.zeros((heads_here, block_len), jnp.float32)
    accum_all = jnp.zeros((block_len, heads_here, HEAD_DIM), jnp.float32)
    return (top_all, total_all, accum_all)


def normalize(state_end):
    top_all, total_all, accum_all = state_end
    return (accum_all / jnp.transpose(total_all)[:, :, None]).astype(jnp.bfloat16)


def per_device(queries, keys, values, block_lists):
    row_count, col_count = queries.shape
    n_head = lax.axis_size("head")
    n_sub = lax.axis_size("sub")
    blk_index = lax.axis_index("blk")
    head_index = lax.axis_index("head")
    sub_index = lax.axis_index("sub")
    tile_total = block_lists.shape[1]
    heads_here = HEADS // (n_head * n_sub)
    block_len = row_count * n_head * n_sub

    def inward(tensor):
        return tensor.reshape(1, 1, row_count, n_head, n_sub, heads_here * HEAD_DIM)

    query_six, keys_six, values_six = (
        lax.all_to_all(
            lax.all_to_all(inward(queries), "head", split_axis=3, concat_axis=1, tiled=True),
            "sub",
            split_axis=4,
            concat_axis=0,
            tiled=True,
        ),
        lax.all_to_all(
            lax.all_to_all(inward(keys), "head", split_axis=3, concat_axis=1, tiled=True),
            "sub",
            split_axis=4,
            concat_axis=0,
            tiled=True,
        ),
        lax.all_to_all(
            lax.all_to_all(inward(values), "head", split_axis=3, concat_axis=1, tiled=True),
            "sub",
            split_axis=4,
            concat_axis=0,
            tiled=True,
        ),
    )
    query_local = query_six.reshape(block_len, heads_here, HEAD_DIM)
    keys_local = keys_six.reshape(block_len, heads_here, HEAD_DIM)
    values_local = values_six.reshape(block_len, heads_here, HEAD_DIM)

    def key_token(positions):
        source_dev = positions // block_len
        within = positions % block_len
        sub_source = within // (n_head * row_count)
        head_source = within // row_count % n_head
        offset = within % row_count
        return ((source_dev * n_head + head_source) * n_sub + sub_source) * row_count + offset

    query_tokens = key_token(blk_index * block_len + jnp.arange(block_len, dtype=jnp.int32))
    first_head = (head_index * n_sub + sub_index) * heads_here
    listed_rows = query_rows(block_lists, first_head, heads_here, query_tokens)
    fold_step = make_step(query_local, listed_rows, key_token, block_len, tile_total)
    state_end = fold_step(
        start_state(heads_here, block_len),
        (
            lax.all_gather(keys_local, "blk", axis=0, tiled=True),
            lax.all_gather(values_local, "blk", axis=0, tiled=True),
        ),
        jnp.int32(0),
    )
    result_rows = normalize(state_end)
    attended = result_rows.reshape(n_sub, n_head, row_count, 1, 1, heads_here * HEAD_DIM)
    returned = lax.all_to_all(
        lax.all_to_all(attended, "head", split_axis=1, concat_axis=3, tiled=True),
        "sub",
        split_axis=0,
        concat_axis=4,
        tiled=True,
    )
    return returned.reshape(row_count, col_count)


EXACT_COUNTS = tuple(range(12, 21))


def rank_of(rank, n_head, n_sub):
    line_count = n_head * n_sub
    return {
        "blk": rank // line_count,
        "head": rank // n_sub % n_head,
        "sub": rank % n_sub,
    }


def remote_copy(sizes, src, dst, send, recv, rank):
    return pltpu.make_async_remote_copy(
        src_ref=src,
        dst_ref=dst,
        send_sem=send,
        recv_sem=recv,
        device_id=rank_of(rank, sizes[1], sizes[2]),
        device_id_type=pl.DeviceIdType.MESH,
    )


def greet(sizes, rank):
    pl.semaphore_signal(
        pltpu.get_barrier_semaphore(), inc=1,
        device_id=rank_of(rank, sizes[1], sizes[2]),
        device_id_type=pl.DeviceIdType.MESH,
    )


def attend_tile(ids, query, buf):
    score_scale = 1.0 / math.sqrt(HEAD_DIM)
    scores, top = [], None
    for tile in ids:
        s = lax.dot_general(
            query, buf[1, tile], (((1,), (1,)), ((), ())), preferred_element_type=jnp.float32
        ) * score_scale
        scores.append(s)
        top = s if top is None else jnp.maximum(top, s)
    row_top = jnp.max(top, axis=1, keepdims=True)
    total, accum = None, None
    for e, tile in enumerate(ids):
        w = jnp.exp(scores[e] - row_top)
        if e:
            repeat = tile == ids[0]
            for f in range(1, e):
                repeat = jnp.logical_or(repeat, tile == ids[f])
            w = w * jnp.where(repeat, 0.0, 1.0)
        part = jnp.dot(
            w.astype(jnp.bfloat16), buf[2, tile], preferred_element_type=jnp.float32
        )
        total = w if total is None else total + w
        accum = part if accum is None else accum + part
    row_total = jnp.sum(total, axis=1, keepdims=True)
    return (accum / row_total).astype(jnp.bfloat16)


def general_kernel(sizes, entries, stage, list_rows, landed, lists, list_sem, *scratch):
    n_blk, n_head, n_sub = sizes
    line_count = n_head * n_sub
    count = n_blk * line_count
    heads_here = HEADS // count
    far_in = scratch[:heads_here]
    far_out = scratch[heads_here : 2 * heads_here]
    send_sem, recv_sem, local_sem = scratch[2 * heads_here :]
    line = lax.axis_index("head") * n_sub + lax.axis_index("sub")
    me = lax.axis_index("blk") * line_count + line

    def peer(d):
        return (me + d) % count

    def inward(t, a, target, sender):
        return remote_copy(
            sizes, stage.at[t, a * count + target], far_in[a].at[t, sender],
            send_sem.at[t, a, target], recv_sem.at[t, a, sender], target,
        )

    def outward(a, target, sender):
        return remote_copy(
            sizes, far_out[a].at[target], landed.at[a * count + sender],
            send_sem.at[3, a, target], recv_sem.at[3, a, sender], target,
        )

    def own_in(t, a):
        return pltpu.make_async_copy(
            stage.at[t, a * count + me], far_in[a].at[t, me], local_sem.at[t, a]
        )

    def own_out(a):
        return pltpu.make_async_copy(
            far_out[a].at[me], landed.at[a * count + me], local_sem.at[3, a]
        )

    def own_list(a):
        return pltpu.make_async_copy(
            list_rows.at[a * count + me], lists.at[a], list_sem.at[a]
        )

    def greet_all(d, carry):
        greet(sizes, peer(d))
        return carry

    lax.fori_loop(1, count, greet_all, 0)
    for a in range(heads_here):
        own_list(a).start()
    pl.semaphore_wait(pltpu.get_barrier_semaphore(), count - 1)

    for a in range(heads_here):
        def send_in(d, carry, a=a):
            for t in range(3):
                inward(t, a, peer(d), me).start()
            return carry

        lax.fori_loop(1, count, send_in, 0)
        for t in range(3):
            own_in(t, a).start()

    for a in range(heads_here):
        for t in range(3):
            own_in(t, a).wait()

        def arrive(d, carry, a=a):
            for t in range(3):
                inward(t, a, me, peer(d)).wait_recv()
            return carry

        lax.fori_loop(1, count, arrive, 0)
        own_list(a).wait()

        def one(i, a=a):
            ids = [lists[a, i * entries + e] for e in range(entries)]
            far_out[a][i] = attend_tile(ids, far_in[a][0, i], far_in[a])

        def work(d, carry, a=a, one=one):
            one(peer(d))

            @pl.when(d > 1)
            def _():
                outward(a, peer(d - 1), me).start()

            return carry

        lax.fori_loop(1, count, work, 0)
        one(me)
        outward(a, peer(count - 1), me).start()
        own_out(a).start()

    for a in range(heads_here):
        own_out(a).wait()

        def finish(d, carry, a=a):
            for t in range(3):
                inward(t, a, peer(d), me).wait_send()
            outward(a, peer(d), me).wait_send()
            outward(a, me, peer(d)).wait_recv()
            return carry

        lax.fori_loop(1, count, finish, 0)


def general_exchange(sizes, collective_id, queries, keys, values, block_lists, table):
    count = sizes[0] * sizes[1] * sizes[2]
    rows = queries.shape[0]
    block = (rows, HEAD_DIM)
    heads_here = HEADS // count
    stage = jnp.stack(
        [jnp.swapaxes(x.reshape(rows, HEADS, HEAD_DIM), 0, 1) for x in (queries, keys, values)]
    )
    list_rows = block_lists.reshape(HEADS, -1)
    anywhere = pl.BlockSpec(memory_space=pl.ANY)
    dma = pltpu.SemaphoreType.DMA
    scratch = [pltpu.SMEM((heads_here, list_rows.shape[1]), jnp.int32), dma((heads_here,))]
    scratch += [pltpu.VMEM((3, count) + block, jnp.bfloat16)] * heads_here
    scratch += [pltpu.VMEM((count,) + block, jnp.bfloat16)] * heads_here
    scratch += [dma((4, heads_here, count))] * 2 + [dma((4, heads_here))]
    landed = pl.pallas_call(
        functools.partial(general_kernel, sizes, block_lists.shape[2]),
        out_shape=jax.ShapeDtypeStruct((HEADS,) + block, jnp.bfloat16),
        in_specs=[anywhere, anywhere],
        out_specs=anywhere,
        scratch_shapes=scratch,
        compiler_params=pltpu.CompilerParams(
            collective_id=collective_id, has_side_effects=True
        ),
    )(stage, list_rows)
    return jnp.swapaxes(landed, 0, 1).reshape(rows, HEADS * HEAD_DIM)


def split_kernel(sizes, near, q_hbm, k_hbm, v_hbm, table_ref, out_ref, table, stage, q_all, k_all,
                 v_all, near_query, near_kv, near_out, far_in, far_out, landed, local_sem,
                 near_send, near_recv, near_back_send, near_back_recv, hop_send, hop_recv,
                 far_send, far_recv, far_back_send, far_back_recv):
    n_blk, n_head, n_sub = sizes
    line_count = n_head * n_sub
    far = HEADS - near
    near_slots = -(-near // line_count)
    far_slots = -(-far // n_blk)
    score_scale = 1.0 / math.sqrt(HEAD_DIM)

    blk, sub = lax.axis_index("blk"), lax.axis_index("sub")
    line = lax.axis_index("head") * n_sub + sub
    first = blk * line_count
    me = first + line

    def near_number(a, target_line):
        return a * line_count + target_line % n_sub * n_head + target_line // n_sub

    def far_number(a, target_blk):
        mirrored = target_blk + sub % 2 * (n_blk - 1 - 2 * target_blk)
        return a * n_blk + (mirrored + n_blk - 1) % n_blk

    def line_peer(d):
        return (line + d) % line_count

    def blk_peer(d):
        return (blk + d) % n_blk

    def if_near(a, target_line, action):
        pl.when(near_number(a, target_line) < near)(action)

    def if_far(a, target_blk, action):
        pl.when(far_number(a, target_blk) < far)(action)

    def near_inward(t, a, target, sender):
        number = near_number(a, target)
        if t:
            source, slot = stage.at[number, pl.ds(0, 2)], near_kv.at[a, 1, sender]
        else:
            source, slot = stage.at[number, 2], near_query.at[a, sender]
        return remote_copy(
            sizes, source, slot, near_send.at[t, a, target], near_recv.at[t, a, sender],
            first + target,
        )

    def near_outward(a, target, sender):
        return remote_copy(
            sizes, near_out.at[a, target], landed.at[near_number(a, sender)],
            near_back_send.at[a, target], near_back_recv.at[a, sender], first + target,
        )

    def hop(a, direction):
        step = 1 - 2 * direction
        return remote_copy(
            sizes, near_kv.at[a, 1], near_kv.at[a, 1 - step],
            hop_send.at[a, direction], hop_recv.at[a, direction],
            (blk + n_blk + step) % n_blk * line_count + line,
        )

    def each_hop(action, sending):
        up, down = blk < n_blk - 1, blk > 0
        pl.when(up if sending else down)(functools.partial(action, 0))
        pl.when(down if sending else up)(functools.partial(action, 1))

    def far_inward(a, target, sender):
        return remote_copy(
            sizes, stage.at[near + far_number(a, target)], far_in.at[a, sender],
            far_send.at[a, target], far_recv.at[a, sender], target * line_count + line,
        )

    def far_outward(a, target, sender):
        return remote_copy(
            sizes, far_out.at[a, target], landed.at[near + far_number(a, sender)],
            far_back_send.at[a, target], far_back_recv.at[a, sender],
            target * line_count + line,
        )

    table_load = pltpu.make_async_copy(table_ref, table, local_sem.at[0])
    table_load.start()
    sources = ((k_hbm, k_all), (v_hbm, v_all), (q_hbm, q_all))

    def load_head(h, carry):
        where = pl.ds(pl.multiple_of(h * HEAD_DIM, HEAD_DIM), HEAD_DIM)
        for t, (source, held) in enumerate(sources):
            pltpu.make_async_copy(source.at[:, where], held.at[h], local_sem.at[1 + t]).start()
        return carry

    lax.fori_loop(0, HEADS, load_head, 0)
    for d in range(1, line_count):
        greet(sizes, first + line_peer(d))
    for d in range(1, n_blk):
        greet(sizes, blk_peer(d) * line_count + line)

    def clear(edge):
        def clear_tile(i, carry):
            near_kv[i // line_count, edge, i % line_count] = jnp.zeros(
                near_kv.shape[3:], near_kv.dtype
            )
            return carry

        lax.fori_loop(0, near_slots * line_count, clear_tile, 0)

    pl.when(blk == 0)(functools.partial(clear, 0))
    pl.when(blk == n_blk - 1)(functools.partial(clear, 2))
    table_load.wait()
    for t, (source, held) in enumerate(sources):
        pltpu.make_async_copy(landed, held, local_sem.at[1 + t]).wait()
    pl.semaphore_wait(pltpu.get_barrier_semaphore(), line_count + n_blk - 2)

    def put_stage(slot):
        head = table[0, slot]
        for t, source in enumerate((k_all, v_all, q_all)):
            stage[slot, t] = source[head]

    def each_other(count, peer, test, action):
        def one(d, carry):
            test(peer(d), lambda: action(peer(d)))
            return carry

        lax.fori_loop(1, count, one, 0)

    def other_far(a, action):
        each_other(n_blk, blk_peer, functools.partial(if_far, a), action)

    def other_near(a, action):
        each_other(line_count, line_peer, functools.partial(if_near, a), action)

    def stage_far(a):
        def own():
            head = table[0, near + far_number(a, blk)]
            for t, source in enumerate((k_all, v_all, q_all)):
                far_in[a, blk, t] = source[head]

        other_far(a, lambda target: put_stage(near + far_number(a, target)))
        if_far(a, blk, own)

    def stage_near(a):
        def own():
            head = table[0, near_number(a, line)]
            near_kv[a, 1, line, 0] = k_all[head]
            near_kv[a, 1, line, 1] = v_all[head]
            near_query[a, line] = q_all[head]

        other_near(a, lambda target: put_stage(near_number(a, target)))
        if_near(a, line, own)

    def send_far(a):
        other_far(a, lambda target: far_inward(a, target, blk).start())

    def send_near(a):
        for t in (1, 0):
            other_near(a, lambda target, t=t: near_inward(t, a, target, line).start())

    def fill(a, carry):
        pl.when(a < far_slots)(lambda: stage_far(a))
        pl.when(jnp.logical_and(a > 0, a <= near_slots))(lambda: send_near(a - 1))
        pl.when(a < near_slots)(lambda: stage_near(a))
        pl.when(a < far_slots)(lambda: send_far(a))
        return carry

    lax.fori_loop(0, max(near_slots + 1, far_slots), fill, 0)

    def finish_tile(scores, values):
        top = None
        for s in scores:
            top = s if top is None else jnp.maximum(top, s)
        row_top = jnp.max(top, axis=1, keepdims=True)
        total, accum = None, None
        for s, value in zip(scores, values):
            w = jnp.exp(s - row_top)
            part = jnp.dot(
                w.astype(jnp.bfloat16), value(), preferred_element_type=jnp.float32
            )
            total = w if total is None else total + w
            accum = part if accum is None else accum + part
        row_total = jnp.sum(total, axis=1, keepdims=True)
        return (accum / row_total).astype(jnp.bfloat16)

    def score(query, key, bits, place):
        s = lax.dot_general(
            query, key, (((1,), (1,)), ((), ())), preferred_element_type=jnp.float32
        )
        return s * score_scale + jnp.where((bits >> place) % 2 == 1, 0.0, NEG_FLOOR)

    def far_tile(a, source):
        bits = table[8 + source * line_count + line, near + far_number(a, blk)]
        query = far_in[a, source, 2]
        scores = [
            score(query, far_in[a, c, 0], bits, c * line_count + line) for c in range(n_blk)
        ]
        return finish_tile(
            scores, [lambda c=c: far_in[a, c, 1] for c in range(n_blk)]
        )

    def near_tile(a, source):
        bits = table[8 + first + source, near_number(a, line)] * (1 << line_count)
        query = near_query[a, source]
        pairs = [(f, c) for f in (1, 0, 2) for c in range(line_count)]
        scores = [
            score(query, near_kv[a, f, c, 0], bits, first + f * line_count + c) for f, c in pairs
        ]
        return finish_tile(scores, [lambda f=f, c=c: near_kv[a, f, c, 1] for f, c in pairs])

    def near_whole(a):
        def whole():
            def arrive(d, carry):
                near_inward(1, a, line, line_peer(d)).wait_recv()
                return carry

            lax.fori_loop(1, line_count, arrive, 0)
            each_hop(lambda direction: hop(a, direction).start(), True)

        pl.when(a < near_slots)(lambda: if_near(a, line, whole))

    def far_work(a):
        def whole():
            number = far_number(a, blk)

            def arrive(d, carry):
                far_inward(a, blk, blk_peer(d)).wait_recv()
                return carry

            lax.fori_loop(1, n_blk, arrive, 0)

            def work(d, carry):
                result = far_tile(a, blk_peer(d))

                @pl.when(d < n_blk)
                def _():
                    far_out[a, blk_peer(d)] = result

                @pl.when(d == n_blk)
                def _():
                    landed[near + number] = result

                @pl.when(d > 1)
                def _():
                    far_outward(a, blk_peer(d - 1), blk).start()

                return carry

            lax.fori_loop(1, n_blk + 1, work, 0)

        pl.when(a < far_slots)(lambda: if_far(a, blk, whole))

    def first_half(a, carry):
        near_whole(2 * a)
        near_whole(2 * a + 1)
        far_work(a)
        return carry

    lax.fori_loop(0, max(far_slots, -(-near_slots // 2)), first_half, 0)

    def second_half(a, carry):
        def whole():
            number = near_number(a, line)
            each_hop(lambda direction: hop(a, direction).wait_recv(), False)

            def arrive(d, carry):
                near_inward(0, a, line, line_peer(d)).wait_recv()
                return carry

            lax.fori_loop(1, line_count, arrive, 0)

            def work(d, carry):
                result = near_tile(a, line_peer(d))

                @pl.when(d < line_count)
                def _():
                    near_out[a, line_peer(d)] = result

                @pl.when(d == line_count)
                def _():
                    landed[number] = result

                @pl.when(d > 1)
                def _():
                    near_outward(a, line_peer(d - 1), line).start()

                return carry

            lax.fori_loop(1, line_count + 1, work, 0)

        if_near(a, line, whole)
        return carry

    lax.fori_loop(0, near_slots, second_half, 0)

    def finish_far(a, carry):
        def own():
            def sent(d, carry):
                far_outward(a, blk_peer(d), blk).wait_send()
                return carry

            lax.fori_loop(1, n_blk, sent, 0)

        def other(target):
            far_inward(a, target, blk).wait_send()
            far_outward(a, blk, target).wait_recv()

        if_far(a, blk, own)
        other_far(a, other)
        return carry

    def finish_near(a, carry):
        def own():
            def sent(d, carry):
                near_outward(a, line_peer(d), line).wait_send()
                return carry

            lax.fori_loop(1, line_count, sent, 0)
            each_hop(lambda direction: hop(a, direction).wait_send(), True)

        def other(target):
            near_inward(1, a, target, line).wait_send()
            near_inward(0, a, target, line).wait_send()
            near_outward(a, line, target).wait_recv()

        if_near(a, line, own)
        other_near(a, other)
        return carry

    lax.fori_loop(0, near_slots, finish_near, 0)
    lax.fori_loop(0, far_slots, finish_far, 0)

    def restore(i, carry):
        for e in range(4):
            h = i * 4 + e
            where = pl.ds(pl.multiple_of(h * HEAD_DIM, HEAD_DIM), HEAD_DIM)
            out_ref[:, where] = landed[table[1, h]]
        return carry

    lax.fori_loop(0, HEADS // 4, restore, 0)


def split_exchange(sizes, near, collective_id, queries, keys, values, block_lists, table):
    n_blk, line_count = sizes[0], sizes[1] * sizes[2]
    rows, width = queries.shape
    near_slots = -(-near // line_count)
    far_slots = -(-(HEADS - near) // n_blk)
    block = (rows, HEAD_DIM)
    anywhere = pl.BlockSpec(memory_space=pl.ANY)
    dma = pltpu.SemaphoreType.DMA

    def buffer(*lead):
        return pltpu.VMEM(lead + block, jnp.bfloat16)

    return pl.pallas_call(
        functools.partial(split_kernel, sizes, near),
        out_shape=jax.ShapeDtypeStruct((rows, width), jnp.bfloat16),
        in_specs=[anywhere] * 4,
        out_specs=pl.BlockSpec(memory_space=pltpu.VMEM),
        scratch_shapes=[
            pltpu.SMEM(table.shape, jnp.int32),
            buffer(HEADS, 3),
            buffer(HEADS),
            buffer(HEADS),
            buffer(HEADS),
            buffer(near_slots, line_count),
            buffer(near_slots, 3, line_count, 2),
            buffer(near_slots, line_count),
            buffer(far_slots, n_blk, 3),
            buffer(far_slots, n_blk),
            buffer(HEADS),
            dma((4,)),
            dma((2, near_slots, line_count)),
            dma((2, near_slots, line_count)),
            dma((near_slots, line_count)),
            dma((near_slots, line_count)),
            dma((near_slots, 2)),
            dma((near_slots, 2)),
            dma((far_slots, n_blk)),
            dma((far_slots, n_blk)),
            dma((far_slots, n_blk)),
            dma((far_slots, n_blk)),
        ],
        compiler_params=pltpu.CompilerParams(
            collective_id=collective_id, has_side_effects=True
        ),
    )(queries, keys, values, table)


def sort_kernel(frames, line_count, entries, lists_ref, table, choice):
    ids = lists_ref[...]
    steps, heads = ids.shape
    tiles = steps // entries
    per_frame = steps // frames
    away = None
    for f in range(frames):
        part = ids[f * per_frame : (f + 1) * per_frame]
        outside = jnp.logical_or(part < (f - 1) * line_count, part >= (f + 2) * line_count)
        found = jnp.max(jnp.where(outside, 1, 0), axis=0, keepdims=True)
        away = found if away is None else jnp.maximum(away, found)
    row = lax.broadcasted_iota(jnp.int32, (heads, heads), 0)
    col = lax.broadcasted_iota(jnp.int32, (heads, heads), 1)
    away_col = jnp.broadcast_to(away, (heads, heads))
    away_row = jnp.broadcast_to(
        jnp.sum(jnp.where(row == col, away_col, 0), axis=1, keepdims=True), (heads, heads)
    )
    same = away_row == away_col
    ahead = jnp.where(same, jnp.where(row < col, 1, 0), away_col)
    place = jnp.sum(ahead, axis=0, keepdims=True)
    behind = jnp.where(same, jnp.where(col < row, 1, 0), away_row)
    place_of_row = jnp.sum(behind, axis=1, keepdims=True)
    perm = jnp.sum(
        jnp.where(jnp.broadcast_to(place_of_row, (heads, heads)) == col, row, 0),
        axis=0, keepdims=True,
    )
    table[0:1, 0:heads] = perm
    table[1:2, 0:heads] = place
    bits = None
    for e in range(entries):
        bit = jnp.left_shift(1, lists_ref[pl.ds(e, tiles, stride=entries), :])
        bits = bit if bits is None else jnp.bitwise_or(bits, bit)
    picks = jnp.where(jnp.broadcast_to(place, (heads, heads)) == row, 1.0, 0.0).astype(jnp.bfloat16)
    low, high = [
        lax.dot_general(
            part.astype(jnp.float32).astype(jnp.bfloat16), picks, (((1,), (1,)), ((), ())),
            preferred_element_type=jnp.float32,
        ).astype(jnp.int32)
        for part in (jnp.bitwise_and(bits, 255), jnp.right_shift(bits, 8))
    ]
    table[8 : 8 + tiles, 0:heads] = low + high * 256
    near = heads - jnp.sum(away.astype(jnp.float32)).astype(jnp.int32)
    least, most = EXACT_COUNTS[0], EXACT_COUNTS[-1]
    known = jnp.logical_and(near >= least, near <= most)
    choice[0] = jnp.where(known, near - least, most - least + 1)


def sort_heads(line_count, block_lists):
    heads, tiles, entries = block_lists.shape
    by_row = jnp.transpose(block_lists, (1, 2, 0)).reshape(tiles * entries, heads)
    vmem = pl.BlockSpec(memory_space=pltpu.VMEM)
    return pl.pallas_call(
        functools.partial(sort_kernel, tiles // line_count, line_count, entries),
        out_shape=(
            jax.ShapeDtypeStruct((8 + tiles, 128), jnp.int32),
            jax.ShapeDtypeStruct((1,), jnp.int32),
        ),
        in_specs=[vmem],
        out_specs=(vmem, pl.BlockSpec(memory_space=pltpu.SMEM)),
    )(by_row)


def solution(mesh):
    sizes = tuple(mesh.shape[axis] for axis in ("blk", "head", "sub"))
    line_count = sizes[1] * sizes[2]
    count = sizes[0] * line_count

    def body(queries, keys, values, block_lists):
        fits = queries.shape[0] == TILE and HEADS % count == 0 and count <= 16
        if not fits or block_lists.shape[1] != count:
            return per_device(queries, keys, values, block_lists)
        table, choice = sort_heads(line_count, block_lists)
        branches = [
            functools.partial(split_exchange, sizes, n, number)
            for number, n in enumerate(EXACT_COUNTS)
        ]
        branches.append(functools.partial(general_exchange, sizes, len(EXACT_COUNTS)))
        return lax.switch(choice[0], branches, queries, keys, values, block_lists, table)

    spec = P(("grp", "blk", "head", "sub"), None)
    return jax.shard_map(
        body, mesh=mesh, in_specs=(spec, spec, spec, P()), out_specs=spec, check_vma=False
    )
```

time: 86.1 us -> 81.3 us (0.944)
  Pallas kernels: 83.8 us -> 78.2 us
    pallas_call x3 -> x2, Pallas kernels: 83.8 us -> 78.2 us  [the longest x1 76.7 us: split_exchange(): pl.pallas_call(functools.partial(split_kernel, sizes, near), out_shape=ja...]
where the time goes in v1:
time: 81.3 us; the launch traced here: 80.3 us
  Pallas kernels  78.2 us (96%)
  local copies, waits for them, and re-layouts  0.97 us (1%)
    pallas_call x1, Pallas kernels, split_exchange(): pl.pallas_call(functools.partial(split_kernel, sizes, near), out_shape=ja...  76.7 us

profile of v1, /device:TPU:11, one launch (start us, length us, event | category | flops | bytes accessed | tf_op | source)
XLA Modules:
  0.0 80.3 jit_solution(589983351572964157)
XLA Ops:
  0.0 1.5 %shard_map.56 = (s32[24,128]{1,0:T(8,128)S(1)}, s32[1]{0:T(128)}) custom-call(s32[128,32]{1,0:T(8,128)} %bitcast.27), custom_call_target="tpu_custom_call" | custom-call | tf_op jit(solution)/shard_map/pallas_call | solution.py:788
  2.2 77.1 %conditional.1 = (bf16[128,4096]{1,0:T(8,128)(2,1)S(1)}) conditional(s32[]{:T(128)} %bitcast.17, (bf16[128,4096]{1,0:T(8,128)(2,1)}, bf16[128,4096]{1,0:T(8,128)(2,1)}, bf16[128,4096]{1,0:T(8,128)(2,1)}, s32[24,128]{1,0:T(8,128)S(1)}) %tuple.35, (bf16[128,4096]{1,0:T(8,128)(2,1)}, bf16[128,4096]{1,0:T(8,128)(2,1)}, ...), branch_computations={%region_0.0_spmd, %region_1.0_spmd, %region_2.0_spmd, %region_3.0_... | conditional | flops 3145728 | bytes 35750008 | solution.py:814
  2.2 76.7 %branch_6_fun.1 = bf16[128,4096]{1,0:T(8,128)(2,1)S(1)} custom-call(bf16[128,4096]{1,0:T(8,128)(2,1)} %get-tuple-element.120.q_hbm, bf16[128,4096]{1,0:T(8,128)(2,1)} %get-tuple-element.121.k_hbm, bf16[128,4096]{1,0:T(8,128)(2,1)} %get-tuple-element.122.v_hbm, s32[24,128]{1,0:T(8,128)S(1)} %get-tuple-element.123.table_ref), custom_call_target="tpu_custom_call" | custom-call | tf_op jit(solution)/shard_map/cond/branch_6_fun/pallas_call | solution.py:702
  79.3 1.0 %copy.55 = bf16[128,4096]{1,0:T(8,128)(2,1)} copy(bf16[128,4096]{1,0:T(8,128)(2,1)S(1)} %get-tuple-element.158) | data formatting | bytes 2097152
